TPU v7x, 256 devices: a whole 4x4x8 slice. The times are simulated.
256 devices in a mesh: slab: 32 (over y, z), chan: 8 (over x, core).
Axes of the slice: x: 4, y: 4, z: 8, core: 2. Of those that a mesh axis runs over, the one named last changes fastest.
Arguments:
- state_field: bfloat16 [2, 16, 256, 256, 256], P(None, 'chan', 'slab'), may hold values from -6 to 6
- spectral_weights: bfloat16 [16, 16, 64, 32, 2, 64], P(None, None, 'chan', None, None, 'slab'), may hold values from -1 to 1
- channel_shift: bfloat16 [16], P('chan'), may hold values from -3 to 3
Outputs:
- layer_output: bfloat16 [2, 16, 256, 256, 256], P(None, 'chan', 'slab')
All inputs are finite; a program needn't handle non-finite values.
Results may differ from a plain program's by a relative error of at most 0.015.
Values may be sent and summed in bfloat16 or wider, within the bound.
A program may use at most 64 MiB of HBM per device.

v0:
```python
import jax
import jax.numpy as jnp
from jax import lax
from jax.sharding import PartitionSpec as P

NG = 256
KM = 32


def kept_freqs(mode_count, grid_side):
    index = jnp.arange(mode_count, dtype=jnp.int32)
    return jnp.where(index < mode_count // 2, index, index + grid_side - mode_count)


def angles(freq_list, grid_side):
    places = jnp.arange(grid_side, dtype=jnp.int32)
    product = freq_list[:, None] * places[None, :] % grid_side
    return product.astype(jnp.float32) * (2.0 * jnp.pi / grid_side)


def make_tables(grid_side, kept):
    bf = jnp.bfloat16
    fwd_scale = 1.0 / jnp.sqrt(jnp.float32(grid_side))
    inv_scale = 1.0 / jnp.sqrt(jnp.float32(2 * kept))
    z_freqs = jnp.arange(kept, dtype=jnp.int32)
    two_freqs = kept_freqs(2 * kept, grid_side)
    theta_z = angles(z_freqs, grid_side)
    theta_two = angles(two_freqs, grid_side)
    cos_z = jnp.cos(theta_z).T
    sin_z = jnp.sin(theta_z).T
    table_z = (jnp.stack([cos_z, -sin_z], -1) * fwd_scale).astype(bf)
    cos_t = jnp.cos(theta_two).T
    sin_t = jnp.sin(theta_two).T
    table_y = (
        jnp.stack([jnp.stack([cos_t, -sin_t], 1), jnp.stack([sin_t, cos_t], 1)], 0) * fwd_scale
    ).astype(bf)
    table_x = (
        jnp.stack([jnp.stack([cos_t, -sin_t], -1), jnp.stack([sin_t, cos_t], -1)], 1) * fwd_scale
    ).astype(bf)
    cos_m = jnp.cos(theta_two)
    sin_m = jnp.sin(theta_two)
    inv_x = (
        jnp.stack([jnp.stack([cos_m, sin_m], -1), jnp.stack([-sin_m, cos_m], -1)], 1) * inv_scale
    ).astype(bf)
    inv_y = (
        jnp.stack([jnp.stack([cos_m, sin_m], 1), jnp.stack([-sin_m, cos_m], 1)], 0) * inv_scale
    ).astype(bf)
    weight_k = jnp.where(z_freqs == 0, 1.0, 2.0).astype(jnp.float32)[:, None]
    inv_z = (
        jnp.stack([weight_k * jnp.cos(theta_z), -weight_k * jnp.sin(theta_z)], 1) * inv_scale
    ).astype(bf)
    return (table_z, table_y, table_x, inv_x, inv_y, inv_z)


def complex_mix(spec_part, wgt_part):
    f32 = jnp.float32
    spec_re = spec_part[..., 0, :]
    spec_im = spec_part[..., 1, :]
    wgt_re = wgt_part[..., 0, :]
    wgt_im = wgt_part[..., 1, :]
    mixed_re = jnp.einsum(
        "nimkj,iomkj->nomkj", spec_re, wgt_re, preferred_element_type=f32
    ) - jnp.einsum("nimkj,iomkj->nomkj", spec_im, wgt_im, preferred_element_type=f32)
    mixed_im = jnp.einsum(
        "nimkj,iomkj->nomkj", spec_re, wgt_im, preferred_element_type=f32
    ) + jnp.einsum("nimkj,iomkj->nomkj", spec_im, wgt_re, preferred_element_type=f32)
    return jnp.stack([mixed_re, mixed_im], -2)


def on_device(state_field, spectral_weights, channel_shift):
    f32 = jnp.float32
    bf = jnp.bfloat16
    table_z, table_y, table_x, inv_x, inv_y, inv_z = make_tables(NG, KM)
    coef_z = jnp.einsum(
        "bcxyz,zkp->bcxkpy", state_field, table_z, preferred_element_type=f32
    ).astype(bf)
    coef_y = jnp.einsum("bcxkpy,pyqn->bcxkqn", coef_z, table_y, preferred_element_type=f32).astype(
        bf
    )
    spectra = jnp.einsum(
        "bcxkpn,xpmq->bcmkqn",
        lax.all_to_all(coef_y, "slab", split_axis=5, concat_axis=2, tiled=True),
        table_x,
        preferred_element_type=f32,
    ).astype(bf)
    mixed = complex_mix(
        lax.all_to_all(spectra, "chan", split_axis=2, concat_axis=1, tiled=True), spectral_weights
    ).astype(bf)
    mixed_own = lax.all_to_all(mixed, "chan", split_axis=1, concat_axis=2, tiled=True)
    back_x = jnp.einsum("bcmkpn,mpxq->bcxkqn", mixed_own, inv_x, preferred_element_type=f32).astype(
        bf
    )
    back_y = jnp.einsum(
        "bcxkpn,pnqy->bcxkqy",
        lax.all_to_all(back_x, "slab", split_axis=2, concat_axis=5, tiled=True),
        inv_y,
        preferred_element_type=f32,
    ).astype(bf)
    summed = jnp.einsum("bcxkpy,kpz->bcxyz", back_y, inv_z, preferred_element_type=f32)
    shifted = summed + channel_shift.astype(f32)[None, :, None, None, None]
    return jax.nn.gelu(shifted, approximate=False).astype(bf)


def solution(mesh):
    return jax.shard_map(
        on_device,
        mesh=mesh,
        in_specs=(
            P(None, "chan", "slab", None, None),
            P(None, None, "chan", None, None, "slab"),
            P("chan"),
        ),
        out_specs=P(None, "chan", "slab", None, None),
        check_vma=False,
    )
```

profile of v0, /device:TPU:32, one launch (start us, length us, event | category | flops | bytes accessed | tf_op | source)
XLA Modules:
  0.0 108.4 jit_solution(18132922754155085922)
XLA Ops:
  0.0 0.1 sine_negate_fusion
  0.2 0.3 fusion.135
  0.5 3.9 %fusion.26 = bf16[2,2,8,32,2,64]{5,3,4,2,1,0:T(8,128)(2,1)S(1)} fusion(bf16[2,2,8,256,256]{4,3,2,1,0:T(8,128)(2,1)} %param.3, f32[1,256,2,64]{1,3,0,2:T(8,128)S(1)} %get-tuple-element.16, f32[1,256,2,64]{1,3,0,2:T(8,128)S(1)} %get-tuple-element.15, f32[256,32,1]{0,1,2:T(8,128)S(1)} %get-tuple-element.29, f32[256,32,1]{0,1,2:T(8,128)S(1)} %get-tuple-element.30), kind=kOutput, calls=%fused_computation.34 | convolution fusion | flops 403554304 | bytes 4784128 | tf_op jit(solution)/shard_map/bcxkpy,pyqn->bcxkqn/dot_general | solution.py:77
  4.4 1.1 copy.32
  5.5 1.7 %reshape.696 = bf16[32,2,2048]{2,1,0:T(2,128)(2,1)} reshape(bf16[64,2,2,8,2,32]{5,4,3,2,1,0:T(2,128)(2,1)S(1)} %bitcast.194) | data formatting | bytes 524288
  7.2 11.4 %all-to-all-start = ((bf16[32,2,2048]{2,1,0:T(2,128)(2,1)}), bf16[32,2,2048]{2,1,0:T(2,128)(2,1)S(1)}, u32[]{:S(2)}, u32[]{:S(2)}) async-start(bf16[32,2,2048]{2,1,0:T(2,128)(2,1)} %reshape.696), calls=%async_computation | async-start | bytes 524288 | tf_op jit(solution)/shard_map/all_to_all | solution.py:82
  18.6 0.3 fusion.134
  18.9 1.0 fusion.129
  19.9 0.7 maximum_bitcast_fusion.2
  20.6 2.8 %fusion.151 = (bf16[16,16,8,32,1,2]{3,5,4,2,1,0:T(2,128)(2,1)S(1)}, bf16[16,16,8,32,1,2]{3,5,4,2,1,0:T(2,128)(2,1)S(1)}) fusion(bf16[16,16,8,32,2,2]{3,5,4,2,1,0:T(2,128)(2,1)} %param.4), kind=kLoop, calls=%fused_computation.172 | loop fusion | bytes 1048576 | tf_op jit(solution)/shard_map/slice | solution.py:59
  23.4 7.5 %all-to-all-done = bf16[32,2,2048]{2,1,0:T(2,128)(2,1)S(1)} async-done(((bf16[32,2,2048]{2,1,0:T(2,128)(2,1)}), bf16[32,2,2048]{2,1,0:T(2,128)(2,1)S(1)}, u32[]{:S(2)}, u32[]{:S(2)}) %all-to-all-start) | async-done | bytes 262176 | tf_op jit(solution)/shard_map/all_to_all | solution.py:82
  30.9 0.5 reshape.697
  31.4 0.1 copy.33
  31.5 1.4 %fusion.50 = bf16[2,2,64,32,2,2]{2,3,5,1,0,4:T(8,128)(2,1)S(1)} fusion(bf16[2,2,32,8,32,2,2]{4,3,6,2,5,1,0:T(8,128)(2,1)S(1)} %bitcast.204, f32[256,1,64,2]{0,2,1,3:T(8,128)} %get-tuple-element.14, f32[256,1,64,2]{0,2,1,3:T(8,128)} %get-tuple-element.13), kind=kOutput, calls=%fused_computation.46 | convolution fusion | flops 33783808 | bytes 589824 | tf_op jit(solution)/shard_map/bcxkpn,xpmq->bcmkqn/dot_general | solution.py:80
  32.9 0.2 copy.36
  33.2 0.9 reshape.698
  34.1 4.3 %all-to-all-start.1 = ((bf16[8,2,2048]{2,1,0:T(2,128)(2,1)}), bf16[8,2,2048]{2,1,0:T(2,128)(2,1)S(1)}, u32[]{:S(2)}, u32[]{:S(2)}) async-start(bf16[8,2,2048]{2,1,0:T(2,128)(2,1)} %reshape.698), calls=%async_computation.1 | async-start | bytes 131072 | tf_op jit(solution)/shard_map/all_to_all | solution.py:87
  38.4 0.3 fusion.119
  38.7 4.3 %copy.78 = bf16[16,16,8,32,1,2]{1,0,5,3,2,4:T(8,128)(2,1)} copy(bf16[16,16,8,32,1,2]{3,5,4,2,1,0:T(2,128)(2,1)S(1)} %get-tuple-element.6) | data formatting | bytes 524288
  43.0 4.3 %copy.76 = bf16[16,16,8,32,1,2]{1,0,5,3,2,4:T(8,128)(2,1)} copy(bf16[16,16,8,32,1,2]{3,5,4,2,1,0:T(2,128)(2,1)S(1)} %get-tuple-element.5) | data formatting | bytes 524288
  47.3 0.0 all-to-all-done.1
  47.3 0.2 reshape.699
  47.5 0.0 copy-start
  47.5 0.1 copy.93
  47.5 0.1 copy.38
  47.6 0.2 copy.75
  47.9 0.2 copy.77
  48.1 2.3 %fusion.12 = f32[8,32,2,2,16]{4,3,2,1,0:T(2,128)S(1)} fusion(bf16[16,16,8,32,1,2]{1,0,5,3,2,4:T(8,128)(2,1)} %copy.78, bf16[2,16,8,32,1,2]{1,0,5,3,2,4:T(2,128)(2,1)S(1)} %copy.75), kind=kOutput, calls=%fused_computation.23 | convolution fusion | flops 524288 | bytes 360448 | tf_op jit(solution)/shard_map/nimkj,iomkj->nomkj/dot_general | solution.py:64
  50.4 2.3 %fusion.14 = f32[8,32,2,2,16]{4,3,2,1,0:T(2,128)S(1)} fusion(bf16[16,16,8,32,1,2]{1,0,5,3,2,4:T(8,128)(2,1)} %copy.78, bf16[2,16,8,32,1,2]{1,0,5,3,2,4:T(2,128)(2,1)S(1)} %copy.77), kind=kOutput, calls=%fused_computation.25 | convolution fusion | flops 524288 | bytes 360448 | tf_op jit(solution)/shard_map/nimkj,iomkj->nomkj/dot_general | solution.py:63
  52.7 0.0 copy-done
  52.7 0.0 copy-start.1
  52.7 0.7 fusion.45
  53.4 0.7 fusion.42
  54.1 0.0 copy-start.2
  54.1 0.9 pad_maximum_fusion
  55.0 0.6 copy.43
  55.7 0.9 reshape.700
  56.6 4.8 %all-to-all-start.2 = ((bf16[8,2,2048]{2,1,0:T(2,128)(2,1)}), bf16[8,2,2048]{2,1,0:T(2,128)(2,1)S(1)}, u32[]{:S(2)}, u32[]{:S(2)}) async-start(bf16[8,2,2048]{2,1,0:T(2,128)(2,1)} %reshape.700), calls=%async_computation.2 | async-start | bytes 131072 | tf_op jit(solution)/shard_map/all_to_all | solution.py:89
  61.4 0.0 copy-done.1
  61.4 5.6 %all-to-all-done.2 = bf16[8,2,2048]{2,1,0:T(2,128)(2,1)S(1)} async-done(((bf16[8,2,2048]{2,1,0:T(2,128)(2,1)}), bf16[8,2,2048]{2,1,0:T(2,128)(2,1)S(1)}, u32[]{:S(2)}, u32[]{:S(2)}) %all-to-all-start.2) | async-done | bytes 65568 | tf_op jit(solution)/shard_map/all_to_all | solution.py:89
  67.0 0.2 reshape.701
  67.2 0.3 fusion.48
  67.5 1.0 copy.47
  68.4 1.7 %reshape.702 = bf16[32,2,2048]{2,1,0:T(2,128)(2,1)} reshape(bf16[256,2,2,2,2,32]{5,4,3,2,1,0:T(2,128)(2,1)S(1)} %bitcast.195) | data formatting | bytes 524288
  70.2 4.6 %all-to-all-start.3 = ((bf16[32,2,2048]{2,1,0:T(2,128)(2,1)}), bf16[32,2,2048]{2,1,0:T(2,128)(2,1)S(1)}, u32[]{:S(2)}, u32[]{:S(2)}) async-start(bf16[32,2,2048]{2,1,0:T(2,128)(2,1)} %reshape.702), calls=%async_computation.3 | async-start | bytes 524288 | tf_op jit(solution)/shard_map/all_to_all | solution.py:95
  74.7 0.0 copy-done.2
  74.8 0.1 sine_multiply_fusion
  74.9 12.0 %all-to-all-done.3 = bf16[32,2,2048]{2,1,0:T(2,128)(2,1)S(1)} async-done(((bf16[32,2,2048]{2,1,0:T(2,128)(2,1)}), bf16[32,2,2048]{2,1,0:T(2,128)(2,1)S(1)}, u32[]{:S(2)}, u32[]{:S(2)}) %all-to-all-start.3) | async-done | bytes 262176 | tf_op jit(solution)/shard_map/all_to_all | solution.py:95
  86.9 0.5 reshape.703
  87.4 0.3 copy.92
  87.7 0.2 copy.49
  87.9 20.5 %fusion.2 = bf16[2,2,8,256,256]{4,3,2,1,0:T(8,128)(2,1)} fusion(f32[2]{0:T(128)S(1)} %convert_element_type.197, bf16[2,2,8,32,2,64,1]{3,2,5,4,1,0,6:T(8,128)(2,1)S(1)} %bitcast.203, f32[1,64,2,256]{3,1,0,2:T(8,128)S(1)} %get-tuple-element.10, f32[1,64,2,256]{3,1,0,2:T(8,128)S(1)} %get-tuple-element.9, f32[32,1,256]{2,0,1:T(8,128)S(1)} %get-tuple-element.31, ...), kind=kOutput, calls=%fused_computation.3 | convolution fusion | flops 541835264 | bytes 4784136 | tf_op jit(solution)/shard_map/bcxkpy,kpz->bcxyz/dot_general | solution.py:99
  (8 shorter events, 0.1 us)
Async XLA Ops:
  7.2 23.7 %all-to-all-start = ((bf16[32,2,2048]{2,1,0:T(2,128)(2,1)}), bf16[32,2,2048]{2,1,0:T(2,128)(2,1)S(1)}, u32[]{:S(2)}, u32[]{:S(2)}) async-start(bf16[32,2,2048]{2,1,0:T(2,128)(2,1)} %reshape.696), calls=%async_computation | async-start | bytes 524288 | tf_op jit(solution)/shard_map/all_to_all | solution.py:82
  34.1 13.2 %all-to-all-start.1 = ((bf16[8,2,2048]{2,1,0:T(2,128)(2,1)}), bf16[8,2,2048]{2,1,0:T(2,128)(2,1)S(1)}, u32[]{:S(2)}, u32[]{:S(2)}) async-start(bf16[8,2,2048]{2,1,0:T(2,128)(2,1)} %reshape.698), calls=%async_computation.1 | async-start | bytes 131072 | tf_op jit(solution)/shard_map/all_to_all | solution.py:87
  47.5 5.2 %copy-start = (bf16[16,16,8,32,1,2]{1,0,5,3,2,4:T(8,128)(2,1)S(1)}, bf16[16,16,8,32,1,2]{1,0,5,3,2,4:T(8,128)(2,1)}, u32[]{:S(2)}) copy-start(bf16[16,16,8,32,1,2]{1,0,5,3,2,4:T(8,128)(2,1)} %copy.76) | copy-start | bytes 786436
  52.7 8.7 %copy-start.1 = (f32[64,256,1]{1,0,2:T(8,128)S(1)}, f32[64,256,1]{1,0,2:T(8,128)}, u32[]{:S(2)}) copy-start(f32[64,256,1]{1,0,2:T(8,128)} %get-tuple-element.22) | copy-start | bytes 196612
  54.1 20.6 %copy-start.2 = (bf16[2]{0:T(256)(128)(2,1)S(1)}, bf16[2]{0:T(256)(128)(2,1)}, u32[]{:S(2)}) copy-start(bf16[2]{0:T(256)(128)(2,1)} %param.5) | copy-start | bytes 16
  56.6 10.4 %all-to-all-start.2 = ((bf16[8,2,2048]{2,1,0:T(2,128)(2,1)}), bf16[8,2,2048]{2,1,0:T(2,128)(2,1)S(1)}, u32[]{:S(2)}, u32[]{:S(2)}) async-start(bf16[8,2,2048]{2,1,0:T(2,128)(2,1)} %reshape.700), calls=%async_computation.2 | async-start | bytes 131072 | tf_op jit(solution)/shard_map/all_to_all | solution.py:89
  70.2 16.8 %all-to-all-start.3 = ((bf16[32,2,2048]{2,1,0:T(2,128)(2,1)}), bf16[32,2,2048]{2,1,0:T(2,128)(2,1)S(1)}, u32[]{:S(2)}, u32[]{:S(2)}) async-start(bf16[32,2,2048]{2,1,0:T(2,128)(2,1)} %reshape.702), calls=%async_computation.3 | async-start | bytes 524288 | tf_op jit(solution)/shard_map/all_to_all | solution.py:95
where the time goes:
time: 109 us; the launch traced here: 108 us
  matrix products  32.1 us (29%)
  starting transfers between devices  25 us (23%)
  waiting for transfers between devices  25 us (23%)
  local copies, waits for them, and re-layouts  22 us (20%)
  other arithmetic  3.96 us (4%)
    dot_general x1, matrix products, on_device(): jnp.einsum('bcxkpy,kpz->bcxyz', back_y, inv_z, preferred_element_type=f32)  20.5 us
    unnamed x18, local copies, waits for them, and re-layouts  15.6 us
    all_to_all x1, waiting for transfers between devices, on_device(): lax.all_to_all(back_x, 'slab', split_axis=2, concat_axis=5, tiled=True)  12 us
    all_to_all x1, starting transfers between devices, on_device(): lax.all_to_all(coef_y, 'slab', split_axis=5, concat_axis=2, tiled=True)  11.4 us
    all_to_all x1, waiting for transfers between devices, on_device(): lax.all_to_all(coef_y, 'slab', split_axis=5, concat_axis=2, tiled=True)  7.48 us
    all_to_all x1, waiting for transfers between devices, on_device(): lax.all_to_all(mixed, 'chan', split_axis=1, concat_axis=2, tiled=True)  5.59 us
    all_to_all x1, starting transfers between devices, on_device(): lax.all_to_all(mixed, 'chan', split_axis=1, concat_axis=2, tiled=True)  4.8 us
    all_to_all x1, starting transfers between devices, on_device(): lax.all_to_all(back_x, 'slab', split_axis=2, concat_axis=5, tiled=True)  4.56 us
  transfers between devices with their start and end apart: 4, of which 3 were waited for; matrix products, arithmetic and copies ran while one was open for 13% of the time, Pallas kernels for 0%

commit v1 on v0

v1 whole, which is shorter than its diff:
```python
import jax
import jax.numpy as jnp
import ml_dtypes
import numpy as np
from jax import lax
from jax.experimental import pallas as pl
from jax.experimental.pallas import tpu as pltpu
from jax.sharding import PartitionSpec as P

NG = 256
KM = 32
NS = 32
NC = 8
XL = NG // NS
ML = 2 * KM // NC
F32 = jnp.float32
BF = jnp.bfloat16
MESH = pl.DeviceIdType.MESH


def make_tables():
    j = np.arange(NG)
    f2 = np.arange(2 * KM)
    f2 = np.where(f2 < KM, f2, f2 + NG - 2 * KM)
    unit = np.float32(2.0 * np.pi / NG)
    tz = ((np.arange(KM)[:, None] * j[None, :]) % NG).astype(np.float32) * unit
    t2 = ((f2[:, None] * j[None, :]) % NG).astype(np.float32) * unit
    cz, sz = np.cos(tz), np.sin(tz)
    c2, s2 = np.cos(t2), np.sin(t2)
    fwd, inv = 1.0 / 16.0, 1.0 / 8.0

    wz = np.zeros((2, 2, NG, 2, 2, 2, KM), np.float32)
    for b in range(2):
        for c in range(2):
            wz[b, c, :, 0, c, b, :] = cz.T * fwd
            wz[b, c, :, 1, c, b, :] = -sz.T * fwd
    wz = wz.reshape(4 * NG, 256)
    order = np.concatenate([np.arange(0, 2 * KM, 2), np.arange(1, 2 * KM, 2)])
    wy = np.concatenate([c2[order], s2[order]], 0) * fwd
    c8, s8 = c2.reshape(NC, ML, NG), s2.reshape(NC, ML, NG)
    wx = np.zeros((NC, 2, ML, NG, 2), np.float32)
    wx[:, 0, :, :, 0], wx[:, 0, :, :, 1] = c8, s8
    wx[:, 1, :, :, 0], wx[:, 1, :, :, 1] = -s8, c8
    wx = wx.reshape(2 * 2 * KM, 2 * NG) * fwd
    ix = np.zeros((NG, 2, NC, 2, ML), np.float32)
    ct, st = c8.transpose(2, 0, 1), s8.transpose(2, 0, 1)
    ix[:, 0, :, 0], ix[:, 0, :, 1] = ct, -st
    ix[:, 1, :, 0], ix[:, 1, :, 1] = st, ct
    ix = ix.reshape(2 * NG, 2 * 2 * KM) * inv
    iy = np.zeros((2, NG, 2, 2, KM), np.float32)
    for h in range(2):
        ch, sh = c2[h::2].T, s2[h::2].T
        iy[0, :, h, 0], iy[0, :, h, 1] = ch, -sh
        iy[1, :, h, 0], iy[1, :, h, 1] = sh, ch
    iy = iy.reshape(2 * NG, 4 * KM) * inv
    wk = np.where(np.arange(KM) == 0, 1.0, 2.0)[:, None]
    iz = np.zeros((2, 2, 2, 2, 2, KM, NG), np.float32)
    for b in range(2):
        for o in range(2):
            iz[b, o, 0, o, b] = wk * cz * inv
            iz[b, o, 1, o, b] = -wk * sz * inv
    iz = iz.reshape(4, 256, NG)
    ew = np.zeros((KM, 2, 2, 2, KM), np.float32)
    for h in range(2):
        for b in range(2):
            ew[:, h, h, b, :] = np.eye(KM)
    ew = ew.reshape(KM, 256)
    return tuple(np.asarray(t).astype(ml_dtypes.bfloat16) for t in (wz, wy, wx, ix, iy, iz, ew))


def forward_kernel(
    state, w2d, wz, wy, wx, ix, ew, out,
    xbuf, wraw, wzb, wyb, wxb, ixb, ewb, tmp, wtmp, wgt,
    send1, recv1, send2, recv2, send3, recv3, send4, recv4,
    in_sem, tab_sem, ssem, rsem,
):
    slab = lax.axis_index("slab")
    chan = lax.axis_index("chan")

    loads = []
    for at, (src, dst) in enumerate(
        ((wz, wzb), (wy, wyb), (w2d, wraw), (wx, wxb), (ix, ixb), (ew, ewb))
    ):
        loads.append(pltpu.make_async_copy(src, dst, tab_sem.at[at]))
    planes = [
        pltpu.make_async_copy(state.at[:, :, x], xbuf.at[x], in_sem.at[x]) for x in range(XL)
    ]
    loads[0].start()
    planes[0].start()
    loads[1].start()
    for x in range(1, XL):
        planes[x].start()
    for at in range(2, 6):
        loads[at].start()

    barrier = pltpu.get_barrier_semaphore()

    def greet_slab(j, carry):
        pl.semaphore_signal(
            barrier, inc=1, device_id=(lax.rem(slab + j, NS), chan), device_id_type=MESH
        )
        return carry

    def greet_chan(j, carry):
        pl.semaphore_signal(
            barrier, inc=1, device_id=(slab, lax.rem(chan + j, NC)), device_id_type=MESH
        )
        return carry

    lax.fori_loop(1, NS, greet_slab, 0)
    lax.fori_loop(1, NC, greet_chan, 0)

    loads[0].wait()
    loads[1].wait()
    for x in range(XL):
        planes[x].wait()
        four = jnp.concatenate([xbuf[x, b, c] for b in range(2) for c in range(2)], axis=1)
        coef_z = jnp.dot(four, wzb[...], preferred_element_type=F32).astype(BF)
        u = jnp.dot(wyb[...], coef_z, preferred_element_type=F32)
        re = u[:64, :128] + u[64:, 128:]
        im = u[:64, 128:] - u[64:, :128]
        for h in range(2):
            tmp[h, pl.ds(2 * x, NS, stride=16), :] = re[h * NS : (h + 1) * NS]
            tmp[h, pl.ds(2 * x + 1, NS, stride=16), :] = im[h * NS : (h + 1) * NS]
    for h in range(2):
        send1[:, :, h * 128 : (h + 1) * 128] = tmp[h].astype(BF).reshape(NS, 16, 128)

    pl.semaphore_wait(barrier, NS - 1 + NC - 1)

    def slab_exchange(send, recv, at):
        def post(j, carry):
            peer = lax.rem(slab + j, NS)
            pltpu.make_async_remote_copy(
                src_ref=send.at[peer],
                dst_ref=recv.at[slab],
                send_sem=ssem.at[at],
                recv_sem=rsem.at[at],
                device_id=(peer, chan),
                device_id_type=MESH,
            ).start()
            return carry

        lax.fori_loop(1, NS, post, 0)
        recv[slab] = send[slab]

    def chan_exchange(send, recv, at):
        def post(j, carry):
            peer = lax.rem(chan + j, NC)
            pltpu.make_async_remote_copy(
                src_ref=send.at[peer],
                dst_ref=recv.at[chan],
                send_sem=ssem.at[at],
                recv_sem=rsem.at[at],
                device_id=(slab, peer),
                device_id_type=MESH,
            ).start()
            return carry

        lax.fori_loop(1, NC, post, 0)
        recv[chan] = send[chan]

    def finish(send, recv, at, n):
        some = pl.ds(0, n - 1)
        pltpu.make_async_copy(recv.at[some], recv.at[some], rsem.at[at]).wait()

    def finish_send(send, at, n):
        some = pl.ds(0, n - 1)
        pltpu.make_async_copy(send.at[some], send.at[some], ssem.at[at]).wait()

    slab_exchange(send1, recv1, 0)

    loads[2].wait()
    loads[5].wait()

    def lay(i, carry):
        rows = wraw[pl.ds(pl.multiple_of(i * 512, 512), 512), :]
        spread = jnp.dot(rows, ewb[...], preferred_element_type=F32)
        wtmp[0] = spread[:, :128]
        wtmp[1] = spread[:, 128:]
        for o in range(16):
            for q in range(2):
                wgt[i, o, q] = (
                    wtmp[0, pl.ds(o * 32 + 2 * q, ML, stride=4), :]
                    + wtmp[1, pl.ds(o * 32 + 2 * q + 1, ML, stride=4), :]
                )
        return carry

    lax.fori_loop(0, 16, lay, 0)
    loads[3].wait()
    loads[4].wait()

    finish(send1, recv1, 0, NS)
    spectra = jnp.dot(wxb[...], recv1[...].reshape(512, 256), preferred_element_type=F32)
    n0, n1 = spectra[:, :128], spectra[:, 128:]
    send2[:, :, :128] = (
        jnp.concatenate([n0[:, :64], n1[:, :64]], 1).astype(BF).reshape(NC, 16, 128)
    )
    send2[:, :, 128:] = (
        jnp.concatenate([n0[:, 64:], n1[:, 64:]], 1).astype(BF).reshape(NC, 16, 128)
    )
    chan_exchange(send2, recv2, 1)
    finish(send2, recv2, 1, NC)

    ins = recv2[...].astype(F32)
    for half in range(NC):
        outs = []
        for o in (2 * half, 2 * half + 1):
            re = jnp.zeros((ML, 128), F32)
            im = jnp.zeros((ML, 128), F32)
            for i in range(16):
                part = ins[i // 2, :, (i % 2) * 128 : (i % 2 + 1) * 128]
                s_re, s_im = part[:ML], part[ML:]
                w_re, w_im = wgt[i, o, 0], wgt[i, o, 1]
                re = re + (s_re * w_re - s_im * w_im)
                im = im + (s_re * w_im + s_im * w_re)
            outs.append(jnp.concatenate([re, im], 0))
        first, second = outs
        send3[half, :, :128] = jnp.concatenate([first[:, :64], second[:, :64]], 1).astype(BF)
        send3[half, :, 128:] = jnp.concatenate([first[:, 64:], second[:, 64:]], 1).astype(BF)
    chan_exchange(send3, recv3, 2)
    finish(send3, recv3, 2, NC)

    back = jnp.dot(ixb[...], recv3[...].reshape(128, 256), preferred_element_type=F32)
    send4[...] = back.astype(BF).reshape(NS, 16, 256)
    slab_exchange(send4, recv4, 3)
    finish(send4, recv4, 3, NS)
    out[...] = recv4[...]
    finish_send(send1, 0, NS)
    finish_send(send2, 1, NC)
    finish_send(send3, 2, NC)
    finish_send(send4, 3, NS)


def inverse_kernel(shift, back, iy, iz, out, wide):
    x = pl.program_id(0)

    @pl.when(x == 0)
    def _():
        full = back[...].reshape(512, 256)
        wide[0] = full[:, :128].astype(F32)
        wide[1] = full[:, 128:].astype(F32)

    rows = [
        wide[h, pl.ds(2 * x + p, NS, stride=16), :].astype(BF) for h in range(2) for p in range(2)
    ]
    cols = jnp.concatenate(rows, 0)
    u = jnp.dot(iy[...], cols, preferred_element_type=F32).astype(BF)
    lhs = jnp.concatenate([u[:NG], u[NG:]], 1)
    for b in range(2):
        for o in range(2):
            v = jnp.dot(lhs, iz[2 * b + o], preferred_element_type=F32) + shift[o]
            out[b, o, 0] = (0.5 * v * (1.0 + lax.erf(v * np.float32(np.sqrt(0.5))))).astype(BF)


def on_device(state_field, spectral_weights, channel_shift):
    wz, wy, wx, ix, iy, iz, ew = make_tables()
    w2d = spectral_weights.transpose(0, 1, 2, 4, 5, 3).reshape(16 * 16 * ML * 4, KM)
    anywhere = pl.BlockSpec(memory_space=pl.ANY)
    vmem = pl.BlockSpec(memory_space=pltpu.VMEM)
    slots, few = (NS, 16, 256), (NC, 16, 256)
    back = pl.pallas_call(
        forward_kernel,
        out_shape=jax.ShapeDtypeStruct(slots, BF),
        in_specs=[anywhere] * 7,
        out_specs=vmem,
        scratch_shapes=[
            pltpu.VMEM((XL, 2, 2, NG, NG), BF),
            pltpu.VMEM(w2d.shape, BF),
            pltpu.VMEM(wz.shape, BF),
            pltpu.VMEM(wy.shape, BF),
            pltpu.VMEM(wx.shape, BF),
            pltpu.VMEM(ix.shape, BF),
            pltpu.VMEM(ew.shape, BF),
            pltpu.VMEM((2, 512, 128), F32),
            pltpu.VMEM((2, 512, 128), F32),
            pltpu.VMEM((16, 16, 2, ML, 128), F32),
            pltpu.VMEM(slots, BF),
            pltpu.VMEM(slots, BF),
            pltpu.VMEM(few, BF),
            pltpu.VMEM(few, BF),
            pltpu.VMEM(few, BF),
            pltpu.VMEM(few, BF),
            pltpu.VMEM(slots, BF),
            pltpu.VMEM(slots, BF),
            pltpu.SemaphoreType.DMA((XL,)),
            pltpu.SemaphoreType.DMA((6,)),
            pltpu.SemaphoreType.DMA((4,)),
            pltpu.SemaphoreType.DMA((4,)),
        ],
        compiler_params=pltpu.CompilerParams(
            collective_id=0, has_side_effects=True, vmem_limit_bytes=40 * 2**20
        ),
    )(state_field, w2d, wz, wy, wx, ix, ew)
    whole = pl.BlockSpec(memory_space=pltpu.VMEM)
    return pl.pallas_call(
        inverse_kernel,
        out_shape=jax.ShapeDtypeStruct((2, 2, XL, NG, NG), BF),
        grid=(XL,),
        in_specs=[pl.BlockSpec(memory_space=pltpu.SMEM), whole, whole, whole],
        out_specs=pl.BlockSpec((2, 2, 1, NG, NG), lambda x: (0, 0, x, 0, 0)),
        scratch_shapes=[pltpu.VMEM((2, 512, 128), F32)],
        compiler_params=pltpu.CompilerParams(vmem_limit_bytes=40 * 2**20),
    )(channel_shift.astype(F32), back, iy, iz)


def solution(mesh):
    return jax.shard_map(
        on_device,
        mesh=mesh,
        in_specs=(
            P(None, "chan", "slab", None, None),
            P(None, None, "chan", None, None, "slab"),
            P("chan"),
        ),
        out_specs=P(None, "chan", "slab", None, None),
        check_vma=False,
    )
```

time: 109 us -> 53.9 us (0.49)
  the two profiles are of different devices: /device:TPU:32 before, /device:TPU:1 now
where the time goes in v1:
time: 53.9 us; the launch traced here: 53.6 us
  Pallas kernels  44.7 us (83%)
  local copies, waits for them, and re-layouts  8.19 us (15%)
  other arithmetic  0.66 us (1%)
    pallas_call x1, Pallas kernels, on_device(): pl.pallas_call(forward_kernel, out_shape=jax.ShapeDtypeStruct(slots, BF),...  38.4 us
    unnamed x18, local copies, waits for them, and re-layouts  8.19 us
    pallas_call x1, Pallas kernels, on_device(): pl.pallas_call(inverse_kernel, out_shape=jax.ShapeDtypeStruct((2, 2, XL,...  6.38 us

profile of v1, /device:TPU:1, one launch (start us, length us, event | category | flops | bytes accessed | tf_op | source)
XLA Modules:
  0.0 53.6 jit_solution(9862920367013345061)
XLA Ops:
  0.0 0.7 %convert_element_type.3.shift = f32[2]{0:T(128)S(1)} convert(bf16[2]{0:T(256)(128)(2,1)} %param.12) | non-fusion elementwise | flops 2 | bytes 12 | tf_op jit(solution)/shard_map/convert_element_type | solution.py:303
  0.7 0.0 copy-start
  0.7 2.2 %copy-done = bf16[2,2,8,256,256]{4,3,2,1,0:T(8,128)(2,1)S(1)} copy-done((bf16[2,2,8,256,256]{4,3,2,1,0:T(8,128)(2,1)S(1)}, bf16[2,2,8,256,256]{4,3,2,1,0:T(8,128)(2,1)}, u32[]{:S(2)}) %copy-start) | copy-done | bytes 4194328
  2.8 0.0 copy-start.1
  2.8 1.6 %copy-done.1 = bf16[16,16,8,32,2,2]{3,5,4,2,1,0:T(2,128)(2,1)S(1)} copy-done((bf16[16,16,8,32,2,2]{3,5,4,2,1,0:T(2,128)(2,1)S(1)}, bf16[16,16,8,32,2,2]{3,5,4,2,1,0:T(2,128)(2,1)}, u32[]{:S(2)}) %copy-start.1) | copy-done | bytes 524312
  4.4 0.0 copy-start.2
  4.4 1.0 %copy-done.2 = bf16[1024,256]{1,0:T(8,128)(2,1)S(1)} copy-done((bf16[1024,256]{1,0:T(8,128)(2,1)S(1)}, bf16[1024,256]{1,0:T(8,128)(2,1)}, u32[]{:S(2)}) %copy-start.2) | copy-done | bytes 524312
  5.5 0.0 copy-start.4
  5.5 0.9 %copy-done.4 = bf16[512,128]{1,0:T(8,128)(2,1)S(1)} copy-done((bf16[512,128]{1,0:T(8,128)(2,1)S(1)}, bf16[512,128]{1,0:T(8,128)(2,1)}, u32[]{:S(2)}) %copy-start.4) | copy-done | bytes 131096
  6.4 0.0 copy-start.5
  6.4 0.9 %copy-done.5 = bf16[128,512]{1,0:T(8,128)(2,1)S(1)} copy-done((bf16[128,512]{1,0:T(8,128)(2,1)S(1)}, bf16[128,512]{1,0:T(8,128)(2,1)}, u32[]{:S(2)}) %copy-start.5) | copy-done | bytes 131096
  7.3 0.0 copy-start.7
  7.3 0.8 %copy-done.7 = bf16[128,256]{1,0:T(8,128)(2,1)S(1)} copy-done((bf16[128,256]{1,0:T(8,128)(2,1)S(1)}, bf16[128,256]{1,0:T(8,128)(2,1)}, u32[]{:S(2)}) %copy-start.7) | copy-done | bytes 65560
  8.1 0.0 copy-start.8
  8.1 0.7 %copy-done.8 = bf16[32,256]{1,0:T(8,128)(2,1)S(1)} copy-done((bf16[32,256]{1,0:T(8,128)(2,1)S(1)}, bf16[32,256]{1,0:T(8,128)(2,1)}, u32[]{:S(2)}) %copy-start.8) | copy-done | bytes 16408
  8.8 0.0 copy-start.3
  8.8 0.0 copy-start.6
  8.9 38.4 %shard_map.100.back = bf16[32,16,256]{2,1,0:T(8,128)(2,1)S(1)} custom-call(bf16[2,2,8,256,256]{4,3,2,1,0:T(8,128)(2,1)S(1)} %copy-done, bf16[8192,32]{1,0:T(8,128)(2,1)S(1)} %bitcast.3, bf16[1024,256]{1,0:T(8,128)(2,1)S(1)} %copy-done.2, bf16[128,256]{1,0:T(8,128)(2,1)S(1)} %copy-done.7, bf16[128,512]{1,0:T(8,128)(2,1)S(1)} %copy-done.5, ...), custom_call_target="tpu_custom_call" | custom-call | tf_op jit(solution)/shard_map/pallas_call | solution.py:261
  47.2 0.0 copy-done.3
  47.2 0.0 copy-done.6
  47.2 6.4 %shard_map.101 = bf16[2,2,8,256,256]{4,3,2,1,0:T(8,128)(2,1)} custom-call(f32[2]{0:T(128)S(1)} %convert_element_type.3.shift, bf16[32,16,256]{2,1,0:T(8,128)(2,1)S(1)} %shard_map.100.back, bf16[512,128]{1,0:T(8,128)(2,1)S(1)} %copy-done.6, bf16[4,256,256]{2,1,0:T(8,128)(2,1)S(1)} %copy-done.3), custom_call_target="tpu_custom_call" | custom-call | tf_op jit(solution)/shard_map/pallas_call | solution.py:295
Async XLA Ops:
  0.7 2.2 %copy-start = (bf16[2,2,8,256,256]{4,3,2,1,0:T(8,128)(2,1)S(1)}, bf16[2,2,8,256,256]{4,3,2,1,0:T(8,128)(2,1)}, u32[]{:S(2)}) copy-start(bf16[2,2,8,256,256]{4,3,2,1,0:T(8,128)(2,1)} %state.1) | copy-start | bytes 12582916
  2.8 1.6 %copy-start.1 = (bf16[16,16,8,32,2,2]{3,5,4,2,1,0:T(2,128)(2,1)S(1)}, bf16[16,16,8,32,2,2]{3,5,4,2,1,0:T(2,128)(2,1)}, u32[]{:S(2)}) copy-start(bf16[16,16,8,32,2,2]{3,5,4,2,1,0:T(2,128)(2,1)} %param.11) | copy-start | bytes 1572868
  4.4 1.0 %copy-start.2 = (bf16[1024,256]{1,0:T(8,128)(2,1)S(1)}, bf16[1024,256]{1,0:T(8,128)(2,1)}, u32[]{:S(2)}) copy-start(bf16[1024,256]{1,0:T(8,128)(2,1)} %constant.14.clone.wz) | copy-start | bytes 1572868
  5.5 0.9 %copy-start.4 = (bf16[512,128]{1,0:T(8,128)(2,1)S(1)}, bf16[512,128]{1,0:T(8,128)(2,1)}, u32[]{:S(2)}) copy-start(bf16[512,128]{1,0:T(8,128)(2,1)} %constant.17.clone.ix) | copy-start | bytes 393220
  6.4 0.9 %copy-start.5 = (bf16[128,512]{1,0:T(8,128)(2,1)S(1)}, bf16[128,512]{1,0:T(8,128)(2,1)}, u32[]{:S(2)}) copy-start(bf16[128,512]{1,0:T(8,128)(2,1)} %constant.16.clone.wx) | copy-start | bytes 393220
  7.3 0.8 %copy-start.7 = (bf16[128,256]{1,0:T(8,128)(2,1)S(1)}, bf16[128,256]{1,0:T(8,128)(2,1)}, u32[]{:S(2)}) copy-start(bf16[128,256]{1,0:T(8,128)(2,1)} %constant.15.clone.wy) | copy-start | bytes 196612
  8.1 0.7 %copy-start.8 = (bf16[32,256]{1,0:T(8,128)(2,1)S(1)}, bf16[32,256]{1,0:T(8,128)(2,1)}, u32[]{:S(2)}) copy-start(bf16[32,256]{1,0:T(8,128)(2,1)} %constant.18.clone.ew) | copy-start | bytes 49156
  8.8 38.4 %copy-start.3 = (bf16[4,256,256]{2,1,0:T(8,128)(2,1)S(1)}, bf16[4,256,256]{2,1,0:T(8,128)(2,1)}, u32[]{:S(2)}) copy-start(bf16[4,256,256]{2,1,0:T(8,128)(2,1)} %constant.20.clone.iz) | copy-start | bytes 1572868
  8.8 38.4 %copy-start.6 = (bf16[512,128]{1,0:T(8,128)(2,1)S(1)}, bf16[512,128]{1,0:T(8,128)(2,1)}, u32[]{:S(2)}) copy-start(bf16[512,128]{1,0:T(8,128)(2,1)} %constant.19.clone.iy) | copy-start | bytes 393220

commit v2 on v1

--- a/solution.py
+++ b/solution.py
@@ -16,6 +16,10 @@
 F32 = jnp.float32
 BF = jnp.bfloat16
 MESH = pl.DeviceIdType.MESH
+STEPS = sorted(
+    ((dy, dz) for dy in range(-1, 3) for dz in range(-3, 5) if (dy, dz) != (0, 0)),
+    key=lambda t: (-abs(t[0]), -abs(t[1]), t[1], t[0]),
+)
 
 
 def make_tables():
@@ -128,8 +132,8 @@
     pl.semaphore_wait(barrier, NS - 1 + NC - 1)
 
     def slab_exchange(send, recv, at):
-        def post(j, carry):
-            peer = lax.rem(slab + j, NS)
+        for dy, dz in STEPS:
+            peer = lax.rem(slab // 8 + dy + 4, 4) * 8 + lax.rem(lax.rem(slab, 8) + dz + 8, 8)
             pltpu.make_async_remote_copy(
                 src_ref=send.at[peer],
                 dst_ref=recv.at[slab],
@@ -138,9 +142,6 @@
                 device_id=(peer, chan),
                 device_id_type=MESH,
             ).start()
-            return carry
-
-        lax.fori_loop(1, NS, post, 0)
         recv[slab] = send[slab]
 
     def chan_exchange(send, recv, at):
@@ -255,9 +256,10 @@
 def on_device(state_field, spectral_weights, channel_shift):
     wz, wy, wx, ix, iy, iz, ew = make_tables()
     w2d = spectral_weights.transpose(0, 1, 2, 4, 5, 3).reshape(16 * 16 * ML * 4, KM)
-    anywhere = pl.BlockSpec(memory_space=pl.ANY)
+    anywhere = pl.BlockSpec(memory_space=pltpu.HBM)
     vmem = pl.BlockSpec(memory_space=pltpu.VMEM)
     slots, few = (NS, 16, 256), (NC, 16, 256)
+    operands = (state_field, w2d, wz, wy, wx, ix, ew)
     back = pl.pallas_call(
         forward_kernel,
         out_shape=jax.ShapeDtypeStruct(slots, BF),
@@ -290,7 +292,7 @@
         compiler_params=pltpu.CompilerParams(
             collective_id=0, has_side_effects=True, vmem_limit_bytes=40 * 2**20
         ),
-    )(state_field, w2d, wz, wy, wx, ix, ew)
+    )(*[pltpu.with_memory_space_constraint(v, pltpu.HBM) for v in operands])
     whole = pl.BlockSpec(memory_space=pltpu.VMEM)
     return pl.pallas_call(
         inverse_kernel,

time: 53.9 us -> 45 us (0.83)
  local copies, waits for them, and re-layouts: 8.19 us -> 0.01 us
    unnamed x18 -> x4, local copies, waits for them, and re-layouts: 8.19 us -> 0.01 us
where the time goes in v2:
time: 45 us
  Pallas kernels  44.2 us (98%)
  other arithmetic  0.72 us (2%)
    pallas_call x1, Pallas kernels, on_device(): pl.pallas_call(forward_kernel, out_shape=jax.ShapeDtypeStruct(slots, BF),...  37.8 us
    pallas_call x1, Pallas kernels, on_device(): pl.pallas_call(inverse_kernel, out_shape=jax.ShapeDtypeStruct((2, 2, XL,...  6.38 us

profile of v2, /device:TPU:1, one launch (start us, length us, event | category | flops | bytes accessed | tf_op | source)
XLA Modules:
  0.0 45.0 jit_solution(7842395178590103241)
XLA Ops:
  0.0 0.0 copy-start
  0.0 0.0 copy-start.1
  0.0 0.7 %convert_element_type.3.shift = f32[2]{0:T(128)S(1)} convert(bf16[2]{0:T(256)(128)(2,1)} %param.12) | non-fusion elementwise | flops 2 | bytes 12 | tf_op jit(solution)/shard_map/convert_element_type | solution.py:305
  0.7 37.8 %shard_map.100.back = bf16[32,16,256]{2,1,0:T(8,128)(2,1)S(1)} custom-call(bf16[2,2,8,256,256]{4,3,2,1,0:T(8,128)(2,1)} %state.1, bf16[8192,32]{1,0:T(8,128)(2,1)} %bitcast.3, bf16[1024,256]{1,0:T(8,128)(2,1)} %constant.14.clone.wz, bf16[128,256]{1,0:T(8,128)(2,1)} %constant.15.clone.wy, bf16[128,512]{1,0:T(8,128)(2,1)} %constant.16.clone.wx, ...), custom_call_target="tpu_custom_call" | custom-call | tf_op jit(solution)/shard_map/pallas_call | solution.py:263
  38.6 0.0 copy-done
  38.6 0.0 copy-done.1
  38.6 6.4 %shard_map.101 = bf16[2,2,8,256,256]{4,3,2,1,0:T(8,128)(2,1)} custom-call(f32[2]{0:T(128)S(1)} %convert_element_type.3.shift, bf16[32,16,256]{2,1,0:T(8,128)(2,1)S(1)} %shard_map.100.back, bf16[512,128]{1,0:T(8,128)(2,1)S(1)} %copy-done.1, bf16[4,256,256]{2,1,0:T(8,128)(2,1)S(1)} %copy-done), custom_call_target="tpu_custom_call" | custom-call | tf_op jit(solution)/shard_map/pallas_call | solution.py:297
Async XLA Ops:
  0.0 38.6 %copy-start = (bf16[4,256,256]{2,1,0:T(8,128)(2,1)S(1)}, bf16[4,256,256]{2,1,0:T(8,128)(2,1)}, u32[]{:S(2)}) copy-start(bf16[4,256,256]{2,1,0:T(8,128)(2,1)} %constant.20.clone.iz) | copy-start | bytes 1572868
  0.0 38.6 %copy-start.1 = (bf16[512,128]{1,0:T(8,128)(2,1)S(1)}, bf16[512,128]{1,0:T(8,128)(2,1)}, u32[]{:S(2)}) copy-start(bf16[512,128]{1,0:T(8,128)(2,1)} %constant.19.clone.iy) | copy-start | bytes 393220

commit v3 on v2

v3 whole, which is shorter than its diff:
```python
import jax
import jax.numpy as jnp
import ml_dtypes
import numpy as np
from jax import lax
from jax.experimental import pallas as pl
from jax.experimental.pallas import tpu as pltpu
from jax.sharding import PartitionSpec as P

NG = 256
KM = 32
NS = 32
NC = 8
XL = NG // NS
ML = 2 * KM // NC
F32 = jnp.float32
BF = jnp.bfloat16
MESH = pl.DeviceIdType.MESH
STEPS = sorted(
    ((dy, dz) for dy in range(-1, 3) for dz in range(-3, 5) if (dy, dz) != (0, 0)),
    key=lambda t: (-abs(t[0]), -abs(t[1]), t[1], t[0]),
)


def make_tables():
    j = np.arange(NG)
    f2 = np.arange(2 * KM)
    f2 = np.where(f2 < KM, f2, f2 + NG - 2 * KM)
    unit = np.float32(2.0 * np.pi / NG)
    tz = ((np.arange(KM)[:, None] * j[None, :]) % NG).astype(np.float32) * unit
    t2 = ((f2[:, None] * j[None, :]) % NG).astype(np.float32) * unit
    cz, sz = np.cos(tz), np.sin(tz)
    c2, s2 = np.cos(t2), np.sin(t2)
    fwd, inv = 1.0 / 16.0, 1.0 / 8.0

    wz = np.zeros((2, 2, NG, 2, 2, 2, KM), np.float32)
    for x in range(2):
        for c in range(2):
            wz[x, c, :, 0, x, c, :] = cz.T * fwd
            wz[x, c, :, 1, x, c, :] = -sz.T * fwd
    wz = wz.reshape(4 * NG, 256)
    order = np.concatenate([np.arange(0, 2 * KM, 2), np.arange(1, 2 * KM, 2)])
    wy = np.concatenate([c2[order], s2[order]], 0) * fwd
    c8, s8 = c2.reshape(NC, ML, NG), s2.reshape(NC, ML, NG)
    wx = np.zeros((NC, 2, ML, NG, 2), np.float32)
    wx[:, 0, :, :, 0], wx[:, 0, :, :, 1] = c8, s8
    wx[:, 1, :, :, 0], wx[:, 1, :, :, 1] = -s8, c8
    wx = wx.reshape(2 * 2 * KM, 2 * NG) * fwd
    ix = np.zeros((NG, 2, NC, 2, ML), np.float32)
    ct, st = c8.transpose(2, 0, 1), s8.transpose(2, 0, 1)
    ix[:, 0, :, 0], ix[:, 0, :, 1] = ct, -st
    ix[:, 1, :, 0], ix[:, 1, :, 1] = st, ct
    ix = ix.reshape(2 * NG, 2 * 2 * KM) * inv
    iy = np.zeros((2, NG, 2, 2, KM), np.float32)
    for h in range(2):
        ch, sh = c2[h::2].T, s2[h::2].T
        iy[0, :, h, 0], iy[0, :, h, 1] = ch, -sh
        iy[1, :, h, 0], iy[1, :, h, 1] = sh, ch
    iy = iy.reshape(2 * NG, 4 * KM) * inv
    wk = np.where(np.arange(KM) == 0, 1.0, 2.0)[:, None]
    iz = np.zeros((2, 2, 2, 2, 2, KM, NG), np.float32)
    for x in range(2):
        for o in range(2):
            iz[x, o, 0, x, o] = wk * cz * inv
            iz[x, o, 1, x, o] = -wk * sz * inv
    iz = iz.reshape(4, 256, NG)
    ew = np.zeros((2, KM, 2, 2, 2, KM), np.float32)
    for c in range(2):
        for h in range(2):
            ew[c, :, h, h, c, :] = np.eye(KM)
    ew = ew.reshape(2, KM, 256)
    return tuple(np.asarray(t).astype(ml_dtypes.bfloat16) for t in (wz, wy, wx, ix, iy, iz, ew))


def split_halves(first, second):
    return (
        jnp.concatenate([first[:, :64], second[:, :64]], 1),
        jnp.concatenate([first[:, 64:], second[:, 64:]], 1),
    )


def inverse_pair(pair, wide, iy, iz, shift, put):
    parts = []
    for p in range(2):
        a = wide[pl.ds(4 * pair + p, NS, stride=16), :]
        b = wide[pl.ds(4 * pair + 2 + p, NS, stride=16), :]
        parts.append(split_halves(a, b))
    cols = jnp.concatenate([parts[p][h] for h in range(2) for p in range(2)], 0).astype(BF)
    u = jnp.dot(iy[...], cols, preferred_element_type=F32).astype(BF)
    lhs = jnp.concatenate([u[:NG], u[NG:]], 1)
    for x in range(2):
        for o in range(2):
            v = jnp.dot(lhs, iz[2 * x + o], preferred_element_type=F32) + shift[:, o : o + 1]
            put(o, 2 * pair + x, (0.5 * v * (1.0 + lax.erf(v * np.float32(np.sqrt(0.5))))).astype(BF))


def forward_kernel(
    state, w2d, wz, wy, wx, ix, ew, iy, iz, shift, done0, back1, bias,
    sbuf, xbuf, wraw, wzb, wyb, wxb, ixb, ewb, iyb, izb, tmp, wtmp, wgt,
    send1, recv1, send2, recv2, send3, recv3, send4, recv4, obuf,
    in_sem, tab_sem, out_sem, ssem, rsem,
):
    slab = lax.axis_index("slab")
    chan = lax.axis_index("chan")

    tables = ((wz, wzb), (wy, wyb), (w2d, wraw), (wx, wxb), (ix, ixb), (ew, ewb), (iy, iyb), (iz, izb), (shift, sbuf))
    loads = [pltpu.make_async_copy(src, dst, tab_sem.at[at]) for at, (src, dst) in enumerate(tables)]
    planes = [
        [
            pltpu.make_async_copy(
                state.at[b, c, pl.ds(4 * h, 4)], xbuf.at[b, c, pl.ds(4 * h, 4)], in_sem.at[b, h, c]
            )
            for h in range(2)
            for c in range(2)
        ]
        for b in range(2)
    ]
    loads[0].start()
    for copy in planes[0]:
        copy.start()
    loads[1].start()
    for copy in planes[1]:
        copy.start()
    for at in (2, 5, 3, 4, 6, 7, 8):
        loads[at].start()

    barrier = pltpu.get_barrier_semaphore()

    def greet_slab(j, carry):
        pl.semaphore_signal(
            barrier, inc=1, device_id=(lax.rem(slab + j, NS), chan), device_id_type=MESH
        )
        return carry

    def greet_chan(j, carry):
        pl.semaphore_signal(
            barrier, inc=1, device_id=(slab, lax.rem(chan + j, NC)), device_id_type=MESH
        )
        return carry

    lax.fori_loop(1, NS, greet_slab, 0)
    lax.fori_loop(1, NC, greet_chan, 0)

    def slab_exchange(send, recv, at, b):
        for dy, dz in STEPS:
            peer = lax.rem(slab // 8 + dy + 4, 4) * 8 + lax.rem(lax.rem(slab, 8) + dz + 8, 8)
            pltpu.make_async_remote_copy(
                src_ref=send.at[b, peer],
                dst_ref=recv.at[b, slab],
                send_sem=ssem.at[at, b],
                recv_sem=rsem.at[at, b],
                device_id=(peer, chan),
                device_id_type=MESH,
            ).start()
        recv[b, slab] = send[b, slab]

    def chan_exchange(send, recv, at, b):
        for j in (4, 5, 3, 2, 6, 7, 1):
            peer = lax.rem(chan + j, NC)
            pltpu.make_async_remote_copy(
                src_ref=send.at[b, peer],
                dst_ref=recv.at[b, chan],
                send_sem=ssem.at[at, b],
                recv_sem=rsem.at[at, b],
                device_id=(slab, peer),
                device_id_type=MESH,
            ).start()
        recv[b, chan] = send[b, chan]

    def finish(recv, at, b, n):
        some = recv.at[b, pl.ds(0, n - 1)]
        pltpu.make_async_copy(some, some, rsem.at[at, b]).wait()

    def finish_send(send, at, b, n):
        some = send.at[b, pl.ds(0, n - 1)]
        pltpu.make_async_copy(some, some, ssem.at[at, b]).wait()

    loads[0].wait()
    for b in range(2):
        for h in range(2):
            for copy in planes[b][2 * h : 2 * h + 2]:
                copy.wait()
            if b == 0 and h == 0:
                loads[1].wait()
            for pair in (2 * h, 2 * h + 1):
                four = jnp.concatenate(
                    [xbuf[b, c, 2 * pair + x] for x in range(2) for c in range(2)], axis=1
                )
                coef_z = jnp.dot(four, wzb[...], preferred_element_type=F32).astype(BF)
                u = jnp.dot(wyb[...], coef_z, preferred_element_type=F32)
                re = u[:64, :128] + u[64:, 128:]
                im = u[:64, 128:] - u[64:, :128]
                for q, val in enumerate((re, im)):
                    for x, rows in enumerate(split_halves(val[:NS], val[NS:])):
                        tmp[pl.ds(2 * (2 * pair + x) + q, NS, stride=16), :] = rows
        send1[b] = tmp[...].astype(BF).reshape(NS, 16, 128)
        if b == 0:
            pl.semaphore_wait(barrier, NS - 1 + NC - 1)
        slab_exchange(send1, recv1, 0, b)

    loads[2].wait()
    loads[5].wait()

    def lay(i, carry):
        even = wraw[pl.ds(pl.multiple_of(i * 1024, 512), 512), :]
        odd = wraw[pl.ds(pl.multiple_of(i * 1024 + 512, 512), 512), :]
        spread = jnp.dot(even, ewb[0], preferred_element_type=F32) + jnp.dot(
            odd, ewb[1], preferred_element_type=F32
        )
        wtmp[0] = spread[:, :128]
        wtmp[1] = spread[:, 128:]
        for o in range(16):
            for q in range(2):
                wgt[i, o, q] = (
                    wtmp[0, pl.ds(o * 32 + 2 * q, ML, stride=4), :]
                    + wtmp[1, pl.ds(o * 32 + 2 * q + 1, ML, stride=4), :]
                )
        return carry

    lax.fori_loop(0, NC, lay, 0)
    for at in (3, 4, 6, 7, 8):
        loads[at].wait()

    for b in range(2):
        finish(recv1, 0, b, NS)
        spectra = jnp.dot(wxb[...], recv1[b].reshape(512, 128), preferred_element_type=F32)
        send2[b] = spectra.astype(BF).reshape(NC, 16, 128)
        chan_exchange(send2, recv2, 1, b)

    low = lax.rem(lax.broadcasted_iota(jnp.int32, (2 * ML, 128), 1), 64) < KM
    for b in range(2):
        finish(recv2, 1, b, NC)
        ins = recv2[b].astype(F32)
        for half in range(NC):
            outs = []
            for o in (2 * half, 2 * half + 1):
                re = jnp.zeros((ML, 128), F32)
                im = jnp.zeros((ML, 128), F32)
                for i in range(NC):
                    s_re, s_im = ins[i, :ML], ins[i, ML:]
                    w_re, w_im = wgt[i, o, 0], wgt[i, o, 1]
                    re = re + (s_re * w_re - s_im * w_im)
                    im = im + (s_re * w_im + s_im * w_re)
                both = jnp.concatenate([re, im], 0)
                outs.append(both + pltpu.roll(both, 128 - KM if o % 2 == 0 else KM, 1))
            send3[b, half] = jnp.where(low, outs[0], outs[1]).astype(BF)
        chan_exchange(send3, recv3, 2, b)

    for b in range(2):
        finish(recv3, 2, b, NC)
        back = jnp.dot(ixb[...], recv3[b].reshape(128, 128), preferred_element_type=F32)
        send4[b] = back.astype(BF).reshape(NS, 16, 128)
        slab_exchange(send4, recv4, 3, b)

    bias[...] = sbuf[...].astype(F32)
    finish(recv4, 3, 0, NS)
    tmp[...] = recv4[0].reshape(512, 128).astype(F32)

    def put(o, x, v):
        obuf[o, x] = v

    def result(pair):
        two = pl.ds(2 * pair, 2)
        return pltpu.make_async_copy(obuf.at[:, two], done0.at[:, two], out_sem.at[pair])

    def inverse(pair, carry):
        inverse_pair(pair, tmp, iyb, izb, bias[...], put)
        result(pair).start()
        return carry

    lax.fori_loop(0, XL // 2, inverse, 0)
    finish(recv4, 3, 1, NS)
    back1[...] = recv4[1]
    for b in range(2):
        finish_send(send1, 0, b, NS)
        finish_send(send2, 1, b, NC)
        finish_send(send3, 2, b, NC)
        finish_send(send4, 3, b, NS)
    for pair in range(XL // 2):
        result(pair).wait()


def inverse_kernel(bias, done0, back1, iy, iz, out, tmp, obuf, sem, out_sem):
    half = pltpu.make_async_copy(done0, out.at[0], sem)
    half.start()
    tmp[...] = back1[...].reshape(512, 128).astype(F32)

    def put(o, x, v):
        obuf[o, x] = v

    def result(pair):
        two = pl.ds(2 * pair, 2)
        return pltpu.make_async_copy(obuf.at[:, two], out.at[1, :, two], out_sem.at[pair])

    def inverse(pair, carry):
        inverse_pair(pair, tmp, iy, iz, bias[...], put)
        result(pair).start()
        return carry

    lax.fori_loop(0, XL // 2, inverse, 0)
    for pair in range(XL // 2):
        result(pair).wait()
    half.wait()


def on_device(state_field, spectral_weights, channel_shift):
    wz, wy, wx, ix, iy, iz, ew = make_tables()
    w2d = spectral_weights.transpose(0, 1, 2, 4, 5, 3).reshape(16 * 16 * ML * 4, KM)
    shift = channel_shift.reshape(1, 2)
    anywhere = pl.BlockSpec(memory_space=pltpu.HBM)
    vmem = pl.BlockSpec(memory_space=pltpu.VMEM)
    slots, few = (2, NS, 16, 128), (2, NC, 16, 128)
    planes = (2, XL, NG, NG)
    operands = (state_field, w2d, wz, wy, wx, ix, ew, iy, iz, shift)
    done0, back1, bias = pl.pallas_call(
        forward_kernel,
        out_shape=(
            jax.ShapeDtypeStruct(planes, BF),
            jax.ShapeDtypeStruct(slots[1:], BF),
            jax.ShapeDtypeStruct((1, 2), F32),
        ),
        in_specs=[anywhere] * len(operands),
        out_specs=(anywhere, vmem, vmem),
        scratch_shapes=[
            pltpu.VMEM((1, 2), BF),
            pltpu.VMEM((2, *planes), BF),
            *[pltpu.VMEM(t.shape, BF) for t in (w2d, wz, wy, wx, ix, ew, iy, iz)],
            pltpu.VMEM((512, 128), F32),
            pltpu.VMEM((2, 512, 128), F32),
            pltpu.VMEM((NC, 16, 2, ML, 128), F32),
            *[pltpu.VMEM(s, BF) for s in (slots, slots, few, few, few, few, slots, slots)],
            pltpu.VMEM(planes, BF),
            pltpu.SemaphoreType.DMA((2, 2, 2)),
            pltpu.SemaphoreType.DMA((9,)),
            pltpu.SemaphoreType.DMA((XL // 2,)),
            pltpu.SemaphoreType.DMA((4, 2)),
            pltpu.SemaphoreType.DMA((4, 2)),
        ],
        compiler_params=pltpu.CompilerParams(
            collective_id=0, has_side_effects=True, vmem_limit_bytes=40 * 2**20
        ),
    )(*[pltpu.with_memory_space_constraint(v, pltpu.HBM) for v in operands])
    return pl.pallas_call(
        inverse_kernel,
        out_shape=jax.ShapeDtypeStruct((2, *planes), BF),
        in_specs=[vmem, anywhere, vmem, vmem, vmem],
        out_specs=anywhere,
        scratch_shapes=[
            pltpu.VMEM((512, 128), F32),
            pltpu.VMEM(planes, BF),
            pltpu.SemaphoreType.DMA,
            pltpu.SemaphoreType.DMA((XL // 2,)),
        ],
        compiler_params=pltpu.CompilerParams(vmem_limit_bytes=40 * 2**20),
    )(bias, done0, back1, iy, iz)


def solution(mesh):
    return jax.shard_map(
        on_device,
        mesh=mesh,
        in_specs=(
            P(None, "chan", "slab", None, None),
            P(None, None, "chan", None, None, "slab"),
            P("chan"),
        ),
        out_specs=P(None, "chan", "slab", None, None),
        check_vma=False,
    )
```

time: 45 us -> 37.4 us (0.83)
  Pallas kernels: 44.2 us -> 37.3 us
  other arithmetic: 0.72 us -> 0 us
    pallas_call x2, Pallas kernels: 44.2 us -> 37.3 us  [the longest x1 34.1 us: on_device(): pl.pallas_call(forward_kernel, out_shape=(jax.ShapeDtypeStruct(planes, BF...]
    convert_element_type x1 -> x0, other arithmetic: 0.72 us -> none  [on_device(): channel_shift.astype(F32)]
where the time goes in v3:
time: 37.4 us; the launch traced here: 37.3 us
  Pallas kernels  37.3 us (100%)
    pallas_call x1, Pallas kernels, on_device(): pl.pallas_call(forward_kernel, out_shape=(jax.ShapeDtypeStruct(planes, BF...  34.1 us
    pallas_call x1, Pallas kernels, on_device(): pl.pallas_call(inverse_kernel, out_shape=jax.ShapeDtypeStruct((2, *planes...  3.19 us

profile of v3, /device:TPU:1, one launch (start us, length us, event | category | flops | bytes accessed | tf_op | source)
XLA Modules:
  0.0 37.3 jit_solution(3253305646597396503)
XLA Ops:
  0.0 0.0 copy-start
  0.0 0.0 copy-start.1
  0.0 34.1 %shard_map.100 = (bf16[2,8,256,256]{3,2,1,0:T(8,128)(2,1)S(1)}, bf16[32,16,128]{2,1,0:T(8,128)(2,1)S(1)}, f32[1,2]{1,0:T(1,128)S(1)}) custom-call(bf16[2,2,8,256,256]{4,3,2,1,0:T(8,128)(2,1)} %state.1, bf16[8192,32]{1,0:T(8,128)(2,1)} %bitcast.4, bf16[1024,256]{1,0:T(8,128)(2,1)} %constant.14.clone.wz, bf16[128,256]{1,0:T(8,128)(2,1)} %constant.15.clone.wy, ...), custom_call_target="tpu_custom_call" | custom-call | tf_op jit(solution)/shard_map/pallas_call | solution.py:315
  34.1 0.0 copy-done
  34.1 0.0 copy-done.1
  34.1 3.2 %shard_map.101 = bf16[2,2,8,256,256]{4,3,2,1,0:T(8,128)(2,1)} custom-call(f32[1,2]{1,0:T(1,128)S(1)} %get-tuple-element.8.bias, bf16[2,8,256,256]{3,2,1,0:T(8,128)(2,1)S(1)} %get-tuple-element.9.done0, bf16[32,16,128]{2,1,0:T(8,128)(2,1)S(1)} %get-tuple-element.10.back1, bf16[512,128]{1,0:T(8,128)(2,1)S(1)} %copy-done.1, bf16[4,256,256]{2,1,0:T(8,128)(2,1)S(1)} %copy-done), custom_call_target="tpu_custom_call" | custom-call | tf_op jit(solution)/shard_map/pallas_call | solution.py:343
Async XLA Ops:
  0.0 34.1 %copy-start = (bf16[4,256,256]{2,1,0:T(8,128)(2,1)S(1)}, bf16[4,256,256]{2,1,0:T(8,128)(2,1)}, u32[]{:S(2)}) copy-start(bf16[4,256,256]{2,1,0:T(8,128)(2,1)} %constant.20.clone.iz) | copy-start | bytes 1572868
  0.0 34.1 %copy-start.1 = (bf16[512,128]{1,0:T(8,128)(2,1)S(1)}, bf16[512,128]{1,0:T(8,128)(2,1)}, u32[]{:S(2)}) copy-start(bf16[512,128]{1,0:T(8,128)(2,1)} %constant.19.clone.iy) | copy-start | bytes 393220

commit v4 on v3

--- a/solution.py
+++ b/solution.py
@@ -79,25 +79,39 @@
     )
 
 
-def inverse_pair(pair, wide, iy, iz, shift, put):
-    parts = []
-    for p in range(2):
-        a = wide[pl.ds(4 * pair + p, NS, stride=16), :]
-        b = wide[pl.ds(4 * pair + 2 + p, NS, stride=16), :]
-        parts.append(split_halves(a, b))
-    cols = jnp.concatenate([parts[p][h] for h in range(2) for p in range(2)], 0).astype(BF)
+def inverse(wide, lhs, iy, iz, shift, obuf, sent):
+    cols = []
+    for pair in range(XL // 2):
+        parts = []
+        for p in range(2):
+            a = wide[pl.ds(4 * pair + p, NS, stride=16), :]
+            b = wide[pl.ds(4 * pair + 2 + p, NS, stride=16), :]
+            parts.append(split_halves(a, b))
+        cols.append(jnp.concatenate([parts[p][h] for h in range(2) for p in range(2)], 0))
+    cols = jnp.concatenate(cols, 1).astype(BF)
     u = jnp.dot(iy[...], cols, preferred_element_type=F32).astype(BF)
-    lhs = jnp.concatenate([u[:NG], u[NG:]], 1)
+    for pair in range(XL // 2):
+        for q in range(2):
+            lhs[pair * NG : (pair + 1) * NG, q * 128 : (q + 1) * 128] = u[
+                q * NG : (q + 1) * NG, pair * 128 : (pair + 1) * 128
+            ]
     for x in range(2):
         for o in range(2):
-            v = jnp.dot(lhs, iz[2 * x + o], preferred_element_type=F32) + shift[:, o : o + 1]
-            put(o, 2 * pair + x, (0.5 * v * (1.0 + lax.erf(v * np.float32(np.sqrt(0.5))))).astype(BF))
+            for h in range(2):
+                v = jnp.dot(
+                    lhs[2 * h * NG : 2 * (h + 1) * NG, :], iz[2 * x + o], preferred_element_type=F32
+                )
+                v = v + shift[:, o : o + 1]
+                v = (0.5 * v * (1.0 + lax.erf(v * np.float32(np.sqrt(0.5))))).astype(BF)
+                for at in range(2):
+                    obuf[o, 2 * h + at, x] = v[at * NG : (at + 1) * NG]
+            sent(o, x).start()
 
 
 def forward_kernel(
     state, w2d, wz, wy, wx, ix, ew, iy, iz, shift, done0, back1, bias,
     sbuf, xbuf, wraw, wzb, wyb, wxb, ixb, ewb, iyb, izb, tmp, wtmp, wgt,
-    send1, recv1, send2, recv2, send3, recv3, send4, recv4, obuf,
+    send1, recv1, send2, recv2, send3, recv3, send4, recv4, lhs, obuf,
     in_sem, tab_sem, out_sem, ssem, rsem,
 ):
     slab = lax.axis_index("slab")
@@ -182,12 +196,18 @@
                 copy.wait()
             if b == 0 and h == 0:
                 loads[1].wait()
-            for pair in (2 * h, 2 * h + 1):
-                four = jnp.concatenate(
-                    [xbuf[b, c, 2 * pair + x] for x in range(2) for c in range(2)], axis=1
+            pairs = (2 * h, 2 * h + 1)
+            fours = [
+                jnp.concatenate([xbuf[b, c, 2 * pair + x] for x in range(2) for c in range(2)], 1)
+                for pair in pairs
+            ]
+            coef_z = jnp.dot(
+                jnp.concatenate(fours, 0), wzb[...], preferred_element_type=F32
+            ).astype(BF)
+            for at, pair in enumerate(pairs):
+                u = jnp.dot(
+                    wyb[...], coef_z[at * NG : (at + 1) * NG], preferred_element_type=F32
                 )
-                coef_z = jnp.dot(four, wzb[...], preferred_element_type=F32).astype(BF)
-                u = jnp.dot(wyb[...], coef_z, preferred_element_type=F32)
                 re = u[:64, :128] + u[64:, 128:]
                 im = u[:64, 128:] - u[64:, :128]
                 for q, val in enumerate((re, im)):
@@ -256,19 +276,10 @@
     finish(recv4, 3, 0, NS)
     tmp[...] = recv4[0].reshape(512, 128).astype(F32)
 
-    def put(o, x, v):
-        obuf[o, x] = v
-
-    def result(pair):
-        two = pl.ds(2 * pair, 2)
-        return pltpu.make_async_copy(obuf.at[:, two], done0.at[:, two], out_sem.at[pair])
-
-    def inverse(pair, carry):
-        inverse_pair(pair, tmp, iyb, izb, bias[...], put)
-        result(pair).start()
-        return carry
-
-    lax.fori_loop(0, XL // 2, inverse, 0)
+    def sent(o, x):
+        return pltpu.make_async_copy(obuf.at[o, :, x], done0.at[o, :, x], out_sem.at[o, x])
+
+    inverse(tmp, lhs, iyb, izb, bias[...], obuf, sent)
     finish(recv4, 3, 1, NS)
     back1[...] = recv4[1]
     for b in range(2):
@@ -276,30 +287,23 @@
         finish_send(send2, 1, b, NC)
         finish_send(send3, 2, b, NC)
         finish_send(send4, 3, b, NS)
-    for pair in range(XL // 2):
-        result(pair).wait()
-
-
-def inverse_kernel(bias, done0, back1, iy, iz, out, tmp, obuf, sem, out_sem):
+    for o in range(2):
+        for x in range(2):
+            sent(o, x).wait()
+
+
+def inverse_kernel(bias, done0, back1, iy, iz, out, tmp, lhs, obuf, sem, out_sem):
     half = pltpu.make_async_copy(done0, out.at[0], sem)
     half.start()
     tmp[...] = back1[...].reshape(512, 128).astype(F32)
 
-    def put(o, x, v):
-        obuf[o, x] = v
-
-    def result(pair):
-        two = pl.ds(2 * pair, 2)
-        return pltpu.make_async_copy(obuf.at[:, two], out.at[1, :, two], out_sem.at[pair])
-
-    def inverse(pair, carry):
-        inverse_pair(pair, tmp, iy, iz, bias[...], put)
-        result(pair).start()
-        return carry
-
-    lax.fori_loop(0, XL // 2, inverse, 0)
-    for pair in range(XL // 2):
-        result(pair).wait()
+    def sent(o, x):
+        return pltpu.make_async_copy(obuf.at[o, :, x], out.at[1, o, :, x], out_sem.at[o, x])
+
+    inverse(tmp, lhs, iy, iz, bias[...], obuf, sent)
+    for o in range(2):
+        for x in range(2):
+            sent(o, x).wait()
     half.wait()
 
 
@@ -310,12 +314,12 @@
     anywhere = pl.BlockSpec(memory_space=pltpu.HBM)
     vmem = pl.BlockSpec(memory_space=pltpu.VMEM)
     slots, few = (2, NS, 16, 128), (2, NC, 16, 128)
-    planes = (2, XL, NG, NG)
+    planes, pairs = (2, XL, NG, NG), (2, XL // 2, 2, NG, NG)
     operands = (state_field, w2d, wz, wy, wx, ix, ew, iy, iz, shift)
     done0, back1, bias = pl.pallas_call(
         forward_kernel,
         out_shape=(
-            jax.ShapeDtypeStruct(planes, BF),
+            jax.ShapeDtypeStruct(pairs, BF),
             jax.ShapeDtypeStruct(slots[1:], BF),
             jax.ShapeDtypeStruct((1, 2), F32),
         ),
@@ -329,10 +333,11 @@
             pltpu.VMEM((2, 512, 128), F32),
             pltpu.VMEM((NC, 16, 2, ML, 128), F32),
             *[pltpu.VMEM(s, BF) for s in (slots, slots, few, few, few, few, slots, slots)],
-            pltpu.VMEM(planes, BF),
+            pltpu.VMEM((4 * NG, 256), BF),
+            pltpu.VMEM(pairs, BF),
             pltpu.SemaphoreType.DMA((2, 2, 2)),
             pltpu.SemaphoreType.DMA((9,)),
-            pltpu.SemaphoreType.DMA((XL // 2,)),
+            pltpu.SemaphoreType.DMA((2, 2)),
             pltpu.SemaphoreType.DMA((4, 2)),
             pltpu.SemaphoreType.DMA((4, 2)),
         ],
@@ -342,17 +347,18 @@
     )(*[pltpu.with_memory_space_constraint(v, pltpu.HBM) for v in operands])
     return pl.pallas_call(
         inverse_kernel,
-        out_shape=jax.ShapeDtypeStruct((2, *planes), BF),
+        out_shape=jax.ShapeDtypeStruct((2, *pairs), BF),
         in_specs=[vmem, anywhere, vmem, vmem, vmem],
         out_specs=anywhere,
         scratch_shapes=[
             pltpu.VMEM((512, 128), F32),
-            pltpu.VMEM(planes, BF),
+            pltpu.VMEM((4 * NG, 256), BF),
+            pltpu.VMEM(pairs, BF),
             pltpu.SemaphoreType.DMA,
-            pltpu.SemaphoreType.DMA((XL // 2,)),
+            pltpu.SemaphoreType.DMA((2, 2)),
         ],
         compiler_params=pltpu.CompilerParams(vmem_limit_bytes=40 * 2**20),
-    )(bias, done0, back1, iy, iz)
+    )(bias, done0, back1, iy, iz).reshape(2, *planes)
 
 
 def solution(mesh):

time: 37.4 us -> 36.9 us (0.987)
  Pallas kernels: 37.3 us -> 36.8 us
    pallas_call x2, Pallas kernels: 37.3 us -> 36.8 us  [the longest x1 34.5 us: on_device(): pl.pallas_call(forward_kernel, out_shape=(jax.ShapeDtypeStruct(pairs, BF)...]
where the time goes in v4:
time: 36.9 us; the launch traced here: 36.8 us
  Pallas kernels  36.8 us (100%)
    pallas_call x1, Pallas kernels, on_device(): pl.pallas_call(forward_kernel, out_shape=(jax.ShapeDtypeStruct(pairs, BF)...  34.5 us
    pallas_call x1, Pallas kernels, on_device(): pl.pallas_call(inverse_kernel, out_shape=jax.ShapeDtypeStruct((2, *pairs)...  2.31 us

profile of v4, /device:TPU:1, one launch (start us, length us, event | category | flops | bytes accessed | tf_op | source)
XLA Modules:
  0.0 36.8 jit_solution(15125039835496173775)
XLA Ops:
  0.0 0.0 copy-start
  0.0 0.0 copy-start.1
  0.0 34.5 %shard_map.100 = (bf16[2,4,2,256,256]{4,3,2,1,0:T(8,128)(2,1)S(1)}, bf16[32,16,128]{2,1,0:T(8,128)(2,1)S(1)}, f32[1,2]{1,0:T(1,128)S(1)}) custom-call(bf16[2,2,8,256,256]{4,3,2,1,0:T(8,128)(2,1)} %state.1, bf16[8192,32]{1,0:T(8,128)(2,1)} %bitcast.5, bf16[1024,256]{1,0:T(8,128)(2,1)} %constant.14.clone.wz, bf16[128,256]{1,0:T(8,128)(2,1)} %constant.15.clone.wy, ...), custom_call_target="tpu_custom_call" | custom-call | tf_op jit(solution)/shard_map/pallas_call | solution.py:319
  34.5 0.0 copy-done
  34.5 0.0 copy-done.1
  34.5 2.3 %shard_map.101 = bf16[2,2,4,2,256,256]{5,4,3,2,1,0:T(8,128)(2,1)} custom-call(f32[1,2]{1,0:T(1,128)S(1)} %get-tuple-element.8.bias, bf16[2,4,2,256,256]{4,3,2,1,0:T(8,128)(2,1)S(1)} %get-tuple-element.9.done0, bf16[32,16,128]{2,1,0:T(8,128)(2,1)S(1)} %get-tuple-element.10.back1, bf16[512,128]{1,0:T(8,128)(2,1)S(1)} %copy-done.1, bf16[4,256,256]{2,1,0:T(8,128)(2,1)S(1)} %copy-done), custom_call_target="tpu_custom_call" | custom-call | tf_op jit(solution)/shard_map/pallas_call | solution.py:348
Async XLA Ops:
  0.0 34.5 %copy-start = (bf16[4,256,256]{2,1,0:T(8,128)(2,1)S(1)}, bf16[4,256,256]{2,1,0:T(8,128)(2,1)}, u32[]{:S(2)}) copy-start(bf16[4,256,256]{2,1,0:T(8,128)(2,1)} %constant.20.clone.iz) | copy-start | bytes 1572868
  0.0 34.5 %copy-start.1 = (bf16[512,128]{1,0:T(8,128)(2,1)S(1)}, bf16[512,128]{1,0:T(8,128)(2,1)}, u32[]{:S(2)}) copy-start(bf16[512,128]{1,0:T(8,128)(2,1)} %constant.19.clone.iy) | copy-start | bytes 393220

commit v5 on v4

--- a/solution.py
+++ b/solution.py
@@ -196,18 +196,12 @@
                 copy.wait()
             if b == 0 and h == 0:
                 loads[1].wait()
-            pairs = (2 * h, 2 * h + 1)
-            fours = [
-                jnp.concatenate([xbuf[b, c, 2 * pair + x] for x in range(2) for c in range(2)], 1)
-                for pair in pairs
-            ]
-            coef_z = jnp.dot(
-                jnp.concatenate(fours, 0), wzb[...], preferred_element_type=F32
-            ).astype(BF)
-            for at, pair in enumerate(pairs):
-                u = jnp.dot(
-                    wyb[...], coef_z[at * NG : (at + 1) * NG], preferred_element_type=F32
+            for pair in (2 * h, 2 * h + 1):
+                four = jnp.concatenate(
+                    [xbuf[b, c, 2 * pair + x] for x in range(2) for c in range(2)], axis=1
                 )
+                coef_z = jnp.dot(four, wzb[...], preferred_element_type=F32).astype(BF)
+                u = jnp.dot(wyb[...], coef_z, preferred_element_type=F32)
                 re = u[:64, :128] + u[64:, 128:]
                 im = u[:64, 128:] - u[64:, :128]
                 for q, val in enumerate((re, im)):

time: 36.9 us -> 36.5 us (0.989)
  Pallas kernels: 36.8 us -> 36.4 us
    pallas_call x1, Pallas kernels: 34.5 us -> 34 us  [on_device(): pl.pallas_call(forward_kernel, out_shape=(jax.ShapeDtypeStruct(pairs, BF)...]
where the time goes in v5:
time: 36.5 us; the launch traced here: 36.4 us
  Pallas kernels  36.4 us (100%)
    pallas_call x1, Pallas kernels, on_device(): pl.pallas_call(forward_kernel, out_shape=(jax.ShapeDtypeStruct(pairs, BF)...  34 us
    pallas_call x1, Pallas kernels, on_device(): pl.pallas_call(inverse_kernel, out_shape=jax.ShapeDtypeStruct((2, *pairs)...  2.31 us

profile of v5, /device:TPU:1, one launch (start us, length us, event | category | flops | bytes accessed | tf_op | source)
XLA Modules:
  0.0 36.4 jit_solution(5982737164289108742)
XLA Ops:
  0.0 0.0 copy-start
  0.0 0.0 copy-start.1
  0.0 34.0 %shard_map.100 = (bf16[2,4,2,256,256]{4,3,2,1,0:T(8,128)(2,1)S(1)}, bf16[32,16,128]{2,1,0:T(8,128)(2,1)S(1)}, f32[1,2]{1,0:T(1,128)S(1)}) custom-call(bf16[2,2,8,256,256]{4,3,2,1,0:T(8,128)(2,1)} %state.1, bf16[8192,32]{1,0:T(8,128)(2,1)} %bitcast.5, bf16[1024,256]{1,0:T(8,128)(2,1)} %constant.14.clone.wz, bf16[128,256]{1,0:T(8,128)(2,1)} %constant.15.clone.wy, ...), custom_call_target="tpu_custom_call" | custom-call | tf_op jit(solution)/shard_map/pallas_call | solution.py:313
  34.1 0.0 copy-done
  34.1 0.0 copy-done.1
  34.1 2.3 %shard_map.101 = bf16[2,2,4,2,256,256]{5,4,3,2,1,0:T(8,128)(2,1)} custom-call(f32[1,2]{1,0:T(1,128)S(1)} %get-tuple-element.8.bias, bf16[2,4,2,256,256]{4,3,2,1,0:T(8,128)(2,1)S(1)} %get-tuple-element.9.done0, bf16[32,16,128]{2,1,0:T(8,128)(2,1)S(1)} %get-tuple-element.10.back1, bf16[512,128]{1,0:T(8,128)(2,1)S(1)} %copy-done.1, bf16[4,256,256]{2,1,0:T(8,128)(2,1)S(1)} %copy-done), custom_call_target="tpu_custom_call" | custom-call | tf_op jit(solution)/shard_map/pallas_call | solution.py:342
Async XLA Ops:
  0.0 34.1 %copy-start = (bf16[4,256,256]{2,1,0:T(8,128)(2,1)S(1)}, bf16[4,256,256]{2,1,0:T(8,128)(2,1)}, u32[]{:S(2)}) copy-start(bf16[4,256,256]{2,1,0:T(8,128)(2,1)} %constant.20.clone.iz) | copy-start | bytes 1572868
  0.0 34.1 %copy-start.1 = (bf16[512,128]{1,0:T(8,128)(2,1)S(1)}, bf16[512,128]{1,0:T(8,128)(2,1)}, u32[]{:S(2)}) copy-start(bf16[512,128]{1,0:T(8,128)(2,1)} %constant.19.clone.iy) | copy-start | bytes 393220

commit v6 on v5

--- a/solution.py
+++ b/solution.py
@@ -169,8 +169,8 @@
         recv[b, slab] = send[b, slab]
 
     def chan_exchange(send, recv, at, b):
-        for j in (4, 5, 3, 2, 6, 7, 1):
-            peer = lax.rem(chan + j, NC)
+        for dx, dc in ((2, 1), (2, 0), (1, 1), (3, 1), (1, 0), (3, 0), (0, 1)):
+            peer = lax.rem(chan // 2 + dx, 4) * 2 + lax.rem(chan + dc, 2)
             pltpu.make_async_remote_copy(
                 src_ref=send.at[b, peer],
                 dst_ref=recv.at[b, chan],

time: 36.5 us -> 36.3 us (level)
  no operation moved by 1% of the time
where the time goes in v6:
time: 36.3 us; the launch traced here: 36.2 us
  Pallas kernels  36.2 us (100%)
    pallas_call x1, Pallas kernels, on_device(): pl.pallas_call(forward_kernel, out_shape=(jax.ShapeDtypeStruct(pairs, BF)...  33.9 us
    pallas_call x1, Pallas kernels, on_device(): pl.pallas_call(inverse_kernel, out_shape=jax.ShapeDtypeStruct((2, *pairs)...  2.3 us

profile of v6, /device:TPU:1, one launch (start us, length us, event | category | flops | bytes accessed | tf_op | source)
XLA Modules:
  0.0 36.2 jit_solution(1119757768347823417)
XLA Ops:
  0.0 0.0 copy-start
  0.0 0.0 copy-start.1
  0.0 33.9 %shard_map.100 = (bf16[2,4,2,256,256]{4,3,2,1,0:T(8,128)(2,1)S(1)}, bf16[32,16,128]{2,1,0:T(8,128)(2,1)S(1)}, f32[1,2]{1,0:T(1,128)S(1)}) custom-call(bf16[2,2,8,256,256]{4,3,2,1,0:T(8,128)(2,1)} %state.1, bf16[8192,32]{1,0:T(8,128)(2,1)} %bitcast.5, bf16[1024,256]{1,0:T(8,128)(2,1)} %constant.14.clone.wz, bf16[128,256]{1,0:T(8,128)(2,1)} %constant.15.clone.wy, ...), custom_call_target="tpu_custom_call" | custom-call | tf_op jit(solution)/shard_map/pallas_call | solution.py:313
  33.9 0.0 copy-done
  33.9 0.0 copy-done.1
  33.9 2.3 %shard_map.101 = bf16[2,2,4,2,256,256]{5,4,3,2,1,0:T(8,128)(2,1)} custom-call(f32[1,2]{1,0:T(1,128)S(1)} %get-tuple-element.8.bias, bf16[2,4,2,256,256]{4,3,2,1,0:T(8,128)(2,1)S(1)} %get-tuple-element.9.done0, bf16[32,16,128]{2,1,0:T(8,128)(2,1)S(1)} %get-tuple-element.10.back1, bf16[512,128]{1,0:T(8,128)(2,1)S(1)} %copy-done.1, bf16[4,256,256]{2,1,0:T(8,128)(2,1)S(1)} %copy-done), custom_call_target="tpu_custom_call" | custom-call | tf_op jit(solution)/shard_map/pallas_call | solution.py:342
Async XLA Ops:
  0.0 33.9 %copy-start = (bf16[4,256,256]{2,1,0:T(8,128)(2,1)S(1)}, bf16[4,256,256]{2,1,0:T(8,128)(2,1)}, u32[]{:S(2)}) copy-start(bf16[4,256,256]{2,1,0:T(8,128)(2,1)} %constant.20.clone.iz) | copy-start | bytes 1572868
  0.0 33.9 %copy-start.1 = (bf16[512,128]{1,0:T(8,128)(2,1)S(1)}, bf16[512,128]{1,0:T(8,128)(2,1)}, u32[]{:S(2)}) copy-start(bf16[512,128]{1,0:T(8,128)(2,1)} %constant.19.clone.iy) | copy-start | bytes 393220

commit v7 on v6

--- a/solution.py
+++ b/solution.py
@@ -168,17 +168,24 @@
             ).start()
         recv[b, slab] = send[b, slab]
 
+    chan_peers = [
+        lax.rem(chan // 2 + dx, 4) * 2 + lax.rem(chan + dc, 2)
+        for dx, dc in ((2, 1), (2, 0), (1, 1), (3, 1), (1, 0), (3, 0), (0, 1))
+    ]
+
+    def chan_copy(send, recv, at, b, peer):
+        pltpu.make_async_remote_copy(
+            src_ref=send.at[b, peer],
+            dst_ref=recv.at[b, chan],
+            send_sem=ssem.at[at, b],
+            recv_sem=rsem.at[at, b],
+            device_id=(slab, peer),
+            device_id_type=MESH,
+        ).start()
+
     def chan_exchange(send, recv, at, b):
-        for dx, dc in ((2, 1), (2, 0), (1, 1), (3, 1), (1, 0), (3, 0), (0, 1)):
-            peer = lax.rem(chan // 2 + dx, 4) * 2 + lax.rem(chan + dc, 2)
-            pltpu.make_async_remote_copy(
-                src_ref=send.at[b, peer],
-                dst_ref=recv.at[b, chan],
-                send_sem=ssem.at[at, b],
-                recv_sem=rsem.at[at, b],
-                device_id=(slab, peer),
-                device_id_type=MESH,
-            ).start()
+        for peer in chan_peers:
+            chan_copy(send, recv, at, b, peer)
         recv[b, chan] = send[b, chan]
 
     def finish(recv, at, b, n):
@@ -245,9 +252,10 @@
     for b in range(2):
         finish(recv2, 1, b, NC)
         ins = recv2[b].astype(F32)
-        for half in range(NC):
+        for half in [*chan_peers, chan]:
             outs = []
-            for o in (2 * half, 2 * half + 1):
+            for parity in range(2):
+                o = 2 * half + parity
                 re = jnp.zeros((ML, 128), F32)
                 im = jnp.zeros((ML, 128), F32)
                 for i in range(NC):
@@ -256,9 +264,13 @@
                     re = re + (s_re * w_re - s_im * w_im)
                     im = im + (s_re * w_im + s_im * w_re)
                 both = jnp.concatenate([re, im], 0)
-                outs.append(both + pltpu.roll(both, 128 - KM if o % 2 == 0 else KM, 1))
-            send3[b, half] = jnp.where(low, outs[0], outs[1]).astype(BF)
-        chan_exchange(send3, recv3, 2, b)
+                outs.append(both + pltpu.roll(both, 128 - KM if parity == 0 else KM, 1))
+            both = jnp.where(low, outs[0], outs[1]).astype(BF)
+            if half is chan:
+                recv3[b, chan] = both
+            else:
+                send3[b, half] = both
+                chan_copy(send3, recv3, 2, b, half)
 
     for b in range(2):
         finish(recv3, 2, b, NC)

time: 36.3 us -> 36.5 us (level)
  no operation moved by 1% of the time
where the time goes in v7:
time: 36.5 us
  Pallas kernels  36.4 us (100%)
    pallas_call x1, Pallas kernels, on_device(): pl.pallas_call(forward_kernel, out_shape=(jax.ShapeDtypeStruct(pairs, BF)...  34.1 us
    pallas_call x1, Pallas kernels, on_device(): pl.pallas_call(inverse_kernel, out_shape=jax.ShapeDtypeStruct((2, *pairs)...  2.31 us

profile of v7, /device:TPU:1, one launch (start us, length us, event | category | flops | bytes accessed | tf_op | source)
XLA Modules:
  0.0 36.5 jit_solution(5958615834660192482)
XLA Ops:
  0.0 0.0 copy-start
  0.0 0.0 copy-start.1
  0.0 34.1 %shard_map.100 = (bf16[2,4,2,256,256]{4,3,2,1,0:T(8,128)(2,1)S(1)}, bf16[32,16,128]{2,1,0:T(8,128)(2,1)S(1)}, f32[1,2]{1,0:T(1,128)S(1)}) custom-call(bf16[2,2,8,256,256]{4,3,2,1,0:T(8,128)(2,1)} %state.1, bf16[8192,32]{1,0:T(8,128)(2,1)} %bitcast.5, bf16[1024,256]{1,0:T(8,128)(2,1)} %constant.14.clone.wz, bf16[128,256]{1,0:T(8,128)(2,1)} %constant.15.clone.wy, ...), custom_call_target="tpu_custom_call" | custom-call | tf_op jit(solution)/shard_map/pallas_call | solution.py:325
  34.1 0.0 copy-done
  34.1 0.0 copy-done.1
  34.1 2.3 %shard_map.101 = bf16[2,2,4,2,256,256]{5,4,3,2,1,0:T(8,128)(2,1)} custom-call(f32[1,2]{1,0:T(1,128)S(1)} %get-tuple-element.8.bias, bf16[2,4,2,256,256]{4,3,2,1,0:T(8,128)(2,1)S(1)} %get-tuple-element.9.done0, bf16[32,16,128]{2,1,0:T(8,128)(2,1)S(1)} %get-tuple-element.10.back1, bf16[512,128]{1,0:T(8,128)(2,1)S(1)} %copy-done.1, bf16[4,256,256]{2,1,0:T(8,128)(2,1)S(1)} %copy-done), custom_call_target="tpu_custom_call" | custom-call | tf_op jit(solution)/shard_map/pallas_call | solution.py:354
Async XLA Ops:
  0.0 34.1 %copy-start = (bf16[4,256,256]{2,1,0:T(8,128)(2,1)S(1)}, bf16[4,256,256]{2,1,0:T(8,128)(2,1)}, u32[]{:S(2)}) copy-start(bf16[4,256,256]{2,1,0:T(8,128)(2,1)} %constant.20.clone.iz) | copy-start | bytes 1572868
  0.0 34.1 %copy-start.1 = (bf16[512,128]{1,0:T(8,128)(2,1)S(1)}, bf16[512,128]{1,0:T(8,128)(2,1)}, u32[]{:S(2)}) copy-start(bf16[512,128]{1,0:T(8,128)(2,1)} %constant.19.clone.iy) | copy-start | bytes 393220
